TPU v7x, 32 devices: a whole 2x2x4 slice. The times are simulated.
32 devices in a mesh: rows: 8 (over z, y), code: 4 (over x, core).
Axes of the slice: x: 2, y: 2, z: 4, core: 2. Of those that a mesh axis runs over, the one named last changes fastest.
Arguments:
- embedding_vectors: bfloat16 [3072, 256], P('rows'), may hold values from -45.3125 to 45.3125
- codebook: bfloat16 [65536, 256], P(('code', 'rows')), may hold values from -0.38125 to 0.38125
- weights: float32 [3072], P('rows'), may hold values from 0.6 to 4.2
Outputs:
- gradient: float32 [65536, 256], P(('code', 'rows'))
- load: float32 [65536], P(('code', 'rows'))
All inputs are finite; a program needn't handle non-finite values.
Results may differ from a plain program's by a relative error of at most 0.013.
Values may be sent and summed in bfloat16 or wider, within the bound.
No kernel may reach another device: no remote copies, remote signals or barrier semaphores. Data moves between devices by JAX's collectives and lax.ppermute only.
A program may use at most 128 MiB of HBM per device.

v0:
```python
import jax
import jax.numpy as jnp
from jax import lax
from jax.sharding import PartitionSpec as P

ITERS = 3
sharpness_factor = 2.0


def local(embedding_vectors, codebook, weights):
    code_devices = lax.axis_size("code")
    balance = embedding_vectors.shape[0] / (code_devices * codebook.shape[0])
    similarity_table = sharpness_factor * jnp.einsum(
        "nd,kd->nk",
        embedding_vectors,
        lax.all_gather(codebook, "rows", axis=0, tiled=True),
        preferred_element_type=jnp.float32,
    )
    row_peak = lax.pmax(jnp.max(similarity_table, axis=1), "code")
    power_term = jnp.exp(similarity_table - row_peak[:, None])

    def marginal_per_sample(col_scale):
        return lax.psum(jnp.dot(power_term, col_scale, precision=lax.Precision.HIGHEST), "code")

    col_scale = jnp.ones((power_term.shape[1],), jnp.float32)
    row_scale = weights / marginal_per_sample(col_scale)
    for iteration in range(ITERS):
        partial_cols = jnp.dot(row_scale, power_term, precision=lax.Precision.HIGHEST)
        col_scale = balance / lax.psum(partial_cols, "rows")
        row_scale = weights / marginal_per_sample(col_scale)
    transport_plan = power_term * row_scale[:, None] * col_scale[None, :]
    local_mass = jnp.sum(transport_plan, axis=0)
    partial_aggregates = jnp.einsum(
        "nk,nd->kd",
        transport_plan.astype(jnp.bfloat16),
        embedding_vectors,
        preferred_element_type=jnp.float32,
    )
    codeword_sums, code_mass = (
        lax.psum_scatter(partial_aggregates, "rows", scatter_dimension=0, tiled=True),
        lax.psum_scatter(local_mass, "rows", scatter_dimension=0, tiled=True),
    )
    gradient = (code_mass[:, None] * codebook.astype(jnp.float32) - codeword_sums) / balance
    return (gradient, code_mass / balance)


def solution(mesh):
    placed = (P("rows", None), P(("code", "rows"), None), P("rows"))
    return jax.shard_map(
        local,
        mesh=mesh,
        in_specs=placed,
        out_specs=(P(("code", "rows"), None), P(("code", "rows"))),
        check_vma=False,
    )
```

profile of v0, /device:TPU:0, one launch (start us, length us, event | category | flops | bytes accessed | tf_op | source)
XLA Modules:
  0.0 927.6 jit_solution(9325484149887483975)
XLA Ops:
  7.2 0.7 all-gather.2.cloned.1.call-update
  8.0 129.8 %all-gather.2.cloned.1.call-done = bf16[16384,256]{1,0:T(8,128)(2,1)} async-done(((bf16[2048,256]{1,0:T(8,128)(2,1)}), bf16[16384,256]{1,0:T(8,128)(2,1)}) %all-gather.2.cloned.1.call-update) | async-done | bytes 8388624 | tf_op jit(solution)/shard_map/all_gather | solution.py:16
  137.8 15.2 %fusion.11 = (f32[384]{0:T(512)S(1)}, f32[384,16384]{1,0:T(8,128)}) fusion(bf16[384,256]{1,0:T(8,128)(2,1)S(1)} %copy-done, bf16[16384,256]{1,0:T(8,128)(2,1)} %all-gather.2.cloned.1.call-done), kind=kOutput, calls=%fused_computation.22 | convolution fusion | flops 3233807872 | bytes 33752576 | tf_op jit(solution)/shard_map/nd,kd->nk/dot_general | solution.py:13
  153.0 6.1 pmax.7
  159.1 26.1 %convolution_reduce_fusion.3 = f32[384]{0:T(512)S(1)} fusion(f32[384,16384]{1,0:T(8,128)} %get-tuple-element.5, f32[384]{0:T(512)S(1)} %pmax.7), kind=kOutput, calls=%fused_computation.12 | convolution fusion | flops 81788928 | bytes 25168896 | tf_op jit(solution)/shard_map/dot_general | solution.py:23
  185.2 6.6 psum.49
  191.8 18.6 %fusion.10 = f32[1,16384]{1,0:T(1,128)} fusion(f32[384,1]{0,1:T(1,128)S(1)} %reshape.10, f32[384,16384]{1,0:T(8,128)} %get-tuple-element.5, f32[384]{0:T(512)S(1)} %pmax.7), kind=kOutput, calls=%fused_computation.21 | convolution fusion | flops 81788928 | bytes 25234432 | tf_op jit(solution)/shard_map/dot_general | solution.py:28
  210.5 0.0 all-reduce.8.cloned.1.call-start
  210.6 66.2 %all-reduce.6.cloned.1.call-done = f32[16384]{0:T(1024)} async-done(((f32[16384]{0:T(1024)}), f32[16384]{0:T(1024)}) %all-reduce.6.cloned.1.call-update) | async-done | bytes 65552 | tf_op jit(solution)/shard_map/psum | solution.py:29
  276.8 0.9 broadcast_divide_fusion.2
  277.6 26.2 %convolution_reduce_fusion.2 = f32[384]{0:T(512)S(1)} fusion(f32[16384,1]{0,1:T(1,128)S(1)} %bitcast.20, f32[384,16384]{1,0:T(8,128)} %get-tuple-element.5, f32[384]{0:T(512)S(1)} %pmax.7), kind=kOutput, calls=%fused_computation.11 | convolution fusion | flops 81788928 | bytes 25234432 | tf_op jit(solution)/shard_map/dot_general | solution.py:23
  303.8 5.8 psum.51
  309.7 18.6 %fusion.9 = f32[1,16384]{1,0:T(1,128)} fusion(f32[384,1]{0,1:T(1,128)S(1)} %reshape.14, f32[384,16384]{1,0:T(8,128)} %get-tuple-element.5, f32[384]{0:T(512)S(1)} %pmax.7), kind=kOutput, calls=%fused_computation.20 | convolution fusion | flops 81788928 | bytes 25234432 | tf_op jit(solution)/shard_map/dot_general | solution.py:28
  328.3 0.0 all-reduce.10.cloned.1.call-start
  328.4 68.8 %all-reduce.8.cloned.1.call-done = f32[16384]{0:T(1024)} async-done(((f32[16384]{0:T(1024)}), f32[16384]{0:T(1024)}) %all-reduce.8.cloned.1.call-update) | async-done | bytes 65552 | tf_op jit(solution)/shard_map/psum | solution.py:29
  397.1 0.9 broadcast_divide_fusion.1
  398.0 26.2 %convolution_reduce_fusion.1 = f32[384]{0:T(512)S(1)} fusion(f32[16384,1]{0,1:T(1,128)S(1)} %bitcast.21, f32[384,16384]{1,0:T(8,128)} %get-tuple-element.5, f32[384]{0:T(512)S(1)} %pmax.7), kind=kOutput, calls=%fused_computation.10 | convolution fusion | flops 81788928 | bytes 25234432 | tf_op jit(solution)/shard_map/dot_general | solution.py:23
  424.2 5.9 psum.53
  430.1 18.6 %fusion.8 = f32[1,16384]{1,0:T(1,128)} fusion(f32[384,1]{0,1:T(1,128)S(1)} %reshape.18, f32[384,16384]{1,0:T(8,128)} %get-tuple-element.5, f32[384]{0:T(512)S(1)} %pmax.7), kind=kOutput, calls=%fused_computation.19 | convolution fusion | flops 81788928 | bytes 25234432 | tf_op jit(solution)/shard_map/dot_general | solution.py:28
  448.7 0.0 all-reduce.12.cloned.1.call-start
  448.8 68.8 %all-reduce.10.cloned.1.call-done = f32[16384]{0:T(1024)} async-done(((f32[16384]{0:T(1024)}), f32[16384]{0:T(1024)}) %all-reduce.10.cloned.1.call-update) | async-done | bytes 65552 | tf_op jit(solution)/shard_map/psum | solution.py:29
  517.6 0.9 broadcast_divide_fusion
  518.4 26.2 %convolution_reduce_fusion = f32[384]{0:T(512)S(1)} fusion(f32[16384,1]{0,1:T(1,128)S(1)} %bitcast.16, f32[384,16384]{1,0:T(8,128)} %get-tuple-element.5, f32[384]{0:T(512)S(1)} %pmax.7), kind=kOutput, calls=%fused_computation.9 | convolution fusion | flops 81788928 | bytes 25234432 | tf_op jit(solution)/shard_map/dot_general | solution.py:23
  544.6 5.7 psum.55
  550.3 11.9 %fusion.1 = f32[16384]{0:T(1024)} fusion(f32[16384]{0:T(1024)S(1)} %broadcast_divide_fusion, f32[384]{0:T(512)S(1)} %div.39, f32[384,16384]{1,0:T(8,128)} %get-tuple-element.5, f32[384]{0:T(512)S(1)} %pmax.7), kind=kLoop, calls=%fused_computation.4 | loop fusion | flops 25149440 | bytes 25299968 | tf_op jit(solution)/shard_map/reduce_sum | solution.py:32
  562.3 0.3 reduce-scatter.2.cloned.1.call-start
  562.6 14.9 %fusion.2 = f32[16384,256]{1,0:T(8,128)} fusion(bf16[384,256]{1,0:T(8,128)(2,1)S(1)} %copy-done, f32[16384]{0:T(1024)S(1)} %broadcast_divide_fusion, f32[384]{0:T(512)S(1)} %div.39, f32[384,16384]{1,0:T(8,128)} %get-tuple-element.5, f32[384]{0:T(512)S(1)} %pmax.7), kind=kOutput, calls=%fused_computation.5 | convolution fusion | flops 3246391296 | bytes 42208256 | tf_op jit(solution)/shard_map/nk,nd->kd/dot_general | solution.py:33
  577.6 0.6 dynamic-slice
  578.8 52.3 %all-reduce.12.cloned.1.call-done = f32[16384]{0:T(1024)} async-done(((f32[16384]{0:T(1024)}), f32[16384]{0:T(1024)}) %all-reduce.12.cloned.1.call-update) | async-done | bytes 65552
  631.1 1.3 broadcast_multiply_fusion
  632.4 284.8 %reduce-scatter.2.cloned.1.call-done = f32[2048,256]{1,0:T(8,128)} async-done(((f32[16384,256]{1,0:T(8,128)}), f32[2048,256]{1,0:T(8,128)}) %reduce-scatter.2.cloned.1.call-update) | async-done | bytes 2097168 | tf_op jit(solution)/shard_map/reduce_scatter | solution.py:40
  917.2 3.3 subtract_multiply_fusion
  (22 shorter events, 0.2 us)
Async XLA Ops:
  7.2 130.6 %copy-start = (bf16[384,256]{1,0:T(8,128)(2,1)S(1)}, bf16[384,256]{1,0:T(8,128)(2,1)}, u32[]{:S(2)}) copy-start(bf16[384,256]{1,0:T(8,128)(2,1)} %param.3) | copy-start | bytes 589828
  7.2 130.6 %all-gather.2.cloned.1.call-start = ((), (), s32[]{:S(2)}) async-start(), calls=%async_computation.1 | async-start | bytes 9437184 | tf_op jit(solution)/shard_map/all_gather | solution.py:16
  7.9 183.9 %copy-start.2 = (f32[384]{0:T(512)S(1)}, f32[384]{0:T(512)}, u32[]{:S(2)}) copy-start(f32[384]{0:T(512)} %param.5) | copy-start | bytes 4612
  7.9 268.8 %all-reduce.6.cloned.1.call-start = ((), (), s32[]{:S(2)}) async-start(), calls=%async_computation.2 | async-start | bytes 131072 | tf_op jit(solution)/shard_map/psum | solution.py:29
  210.5 186.6 %all-reduce.8.cloned.1.call-start = ((), (), s32[]{:S(2)}) async-start(), calls=%async_computation.3 | async-start | bytes 131072 | tf_op jit(solution)/shard_map/psum | solution.py:29
  328.3 189.3 %all-reduce.10.cloned.1.call-start = ((), (), s32[]{:S(2)}) async-start(), calls=%async_computation.4 | async-start | bytes 131072 | tf_op jit(solution)/shard_map/psum | solution.py:29
  448.7 182.4 %all-reduce.12.cloned.1.call-start = ((), (), s32[]{:S(2)}) async-start(), calls=%async_computation.6 | async-start | bytes 131072
  562.3 15.3 %copy-start.3 = (u32[32]{0:T(128)S(1)}, u32[32]{0:T(128)}, u32[]{:S(2)}) copy-start(u32[32]{0:T(128)} %constant.17) | copy-start | bytes 388
  562.3 354.9 %copy-start.1 = (bf16[2048,256]{1,0:T(8,128)(2,1)S(1)}, bf16[2048,256]{1,0:T(8,128)(2,1)}, u32[]{:S(2)}) copy-start(bf16[2048,256]{1,0:T(8,128)(2,1)} %param.4) | copy-start | bytes 3145732
  562.3 354.9 %reduce-scatter.2.cloned.1.call-start = ((), (), s32[]{:S(2)}) async-start(), calls=%async_computation.5 | async-start | bytes 18874368 | tf_op jit(solution)/shard_map/reduce_scatter | solution.py:40
Sparse Core Ops, SparseCore 0:
  10.1 127.6 all-gather.1
  210.6 66.0 all-reduce.5
  328.4 68.6 all-reduce.7
  448.9 68.6 all-reduce.9
  562.4 68.6 all-reduce.11
  634.7 282.4 reduce-scatter.1
where the time goes:
time: 935 us; the launch traced here: 928 us
  waiting for transfers between devices  671 us (72%)
  matrix products  191 us (20%)
  blocking collectives  30.1 us (3%)
  other arithmetic  19.1 us (2%)
  between operations  15.1 us (2%)
    reduce_scatter x1, waiting for transfers between devices, local(): lax.psum_scatter(partial_aggregates, 'rows', scatter_dimension=0, tiled=T...  285 us
    psum x3, waiting for transfers between devices, local(): col_scale = balance / lax.psum(partial_cols, 'rows')  204 us
    all_gather x1, waiting for transfers between devices, local(): lax.all_gather(codebook, 'rows', axis=0, tiled=True)  130 us
    dot_general x4, matrix products, marginal_per_sample(): jnp.dot(power_term, col_scale, precision=lax.Precision.HIGHEST)  105 us
    dot_general x3, matrix products, local(): jnp.dot(row_scale, power_term, precision=lax.Precision.HIGHEST)  55.9 us
    unnamed x7, waiting for transfers between devices  53.1 us
    psum x4, blocking collectives, marginal_per_sample(): lax.psum(jnp.dot(power_term, col_scale, precision=lax.Precision.HIGHEST),...  24 us
  transfers between devices with their start and end apart: 6, of which 6 were waited for; matrix products, arithmetic and copies ran while one was open for 2% of the time, Pallas kernels for 0%

commit v1 on v0

--- a/solution.py
+++ b/solution.py
@@ -5,6 +5,11 @@
 
 ITERS = 3
 sharpness_factor = 2.0
+
+
+def add_all(array, axis):
+    pieces = lax.all_gather(array, axis)
+    return jnp.sum(pieces, axis=0)
 
 
 def local(embedding_vectors, codebook, weights):
@@ -26,7 +31,7 @@
     row_scale = weights / marginal_per_sample(col_scale)
     for iteration in range(ITERS):
         partial_cols = jnp.dot(row_scale, power_term, precision=lax.Precision.HIGHEST)
-        col_scale = balance / lax.psum(partial_cols, "rows")
+        col_scale = balance / add_all(partial_cols, "rows")
         row_scale = weights / marginal_per_sample(col_scale)
     transport_plan = power_term * row_scale[:, None] * col_scale[None, :]
     local_mass = jnp.sum(transport_plan, axis=0)

time: 935 us -> 819 us (0.88)
  waiting for transfers between devices: 671 us -> 466 us
  blocking collectives: 30.1 us -> 124 us
    psum x3 -> x0, waiting for transfers between devices: 204 us -> none  [local(): col_scale = balance / lax.psum(partial_cols, 'rows')]
    all_gather x0 -> x3, blocking collectives: none -> 94 us  [add_all(): pieces = lax.all_gather(array, axis)]
    unnamed x7 -> x4, waiting for transfers between devices: 53.1 us -> 51 us
  transfers between devices with their start and end apart: 6 -> 3, of which waited for: 6 -> 3; matrix products, arithmetic and copies ran while one was open for 2% -> 2% of each run, Pallas kernels for 0% -> 0%
where the time goes in v1:
time: 819 us; the launch traced here: 812 us
  waiting for transfers between devices  466 us (57%)
  matrix products  189 us (23%)
  blocking collectives  124 us (15%)
  other arithmetic  17 us (2%)
  between operations  14.8 us (2%)
    reduce_scatter x1, waiting for transfers between devices, local(): lax.psum_scatter(partial_aggregates, 'rows', scatter_dimension=0, tiled=T...  285 us
    all_gather x1, waiting for transfers between devices, local(): lax.all_gather(codebook, 'rows', axis=0, tiled=True)  130 us
    dot_general x4, matrix products, marginal_per_sample(): jnp.dot(power_term, col_scale, precision=lax.Precision.HIGHEST)  105 us
    all_gather x3, blocking collectives, add_all(): pieces = lax.all_gather(array, axis)  94 us
    dot_general x3, matrix products, local(): jnp.dot(row_scale, power_term, precision=lax.Precision.HIGHEST)  54 us
    unnamed x4, waiting for transfers between devices  51 us
    psum x4, blocking collectives, marginal_per_sample(): lax.psum(jnp.dot(power_term, col_scale, precision=lax.Precision.HIGHEST),...  24 us
  transfers between devices with their start and end apart: 3, of which 3 were waited for; matrix products, arithmetic and copies ran while one was open for 2% of the time, Pallas kernels for 0%

profile of v1, /device:TPU:0, one launch (start us, length us, event | category | flops | bytes accessed | tf_op | source)
XLA Modules:
  0.0 811.8 jit_solution(12716565624459927110)
XLA Ops:
  7.2 0.7 all-gather.5.cloned.1.call-update
  8.0 129.8 %all-gather.5.cloned.1.call-done = bf16[16384,256]{1,0:T(8,128)(2,1)} async-done(((bf16[2048,256]{1,0:T(8,128)(2,1)}), bf16[16384,256]{1,0:T(8,128)(2,1)}) %all-gather.5.cloned.1.call-update) | async-done | bytes 8388624 | tf_op jit(solution)/shard_map/all_gather | solution.py:21
  137.8 15.2 %fusion.11 = (f32[384]{0:T(512)S(1)}, f32[384,16384]{1,0:T(8,128)}) fusion(bf16[384,256]{1,0:T(8,128)(2,1)S(1)} %copy-done, bf16[16384,256]{1,0:T(8,128)(2,1)} %all-gather.5.cloned.1.call-done), kind=kOutput, calls=%fused_computation.22 | convolution fusion | flops 3233807872 | bytes 33752576 | tf_op jit(solution)/shard_map/nd,kd->nk/dot_general | solution.py:18
  153.0 6.1 pmax.7
  159.1 26.1 %convolution_reduce_fusion.3 = f32[384]{0:T(512)S(1)} fusion(f32[384,16384]{1,0:T(8,128)} %get-tuple-element.5, f32[384]{0:T(512)S(1)} %pmax.7), kind=kOutput, calls=%fused_computation.12 | convolution fusion | flops 81788928 | bytes 25168896 | tf_op jit(solution)/shard_map/dot_general | solution.py:28
  185.2 6.6 psum.28
  191.8 18.0 %fusion.10 = f32[1,16384]{1,0:T(1,128)S(1)} fusion(f32[384,1]{0,1:T(1,128)S(1)} %reshape.15, f32[384,16384]{1,0:T(8,128)} %get-tuple-element.5, f32[384]{0:T(512)S(1)} %pmax.7), kind=kOutput, calls=%fused_computation.21 | convolution fusion | flops 81788928 | bytes 25234432 | tf_op jit(solution)/shard_map/dot_general | solution.py:33
  209.9 31.2 %all-gather = f32[131072]{0:T(1024)S(1)} all-gather(f32[16384]{0:T(1024)S(1)} %bitcast.17), channel_id=2, replica_groups=mesh['rows'=8,'code'=4] {'rows'}, dimensions={0}, use_global_device_ids=true | all-gather | bytes 589824 | tf_op jit(solution)/shard_map/all_gather | solution.py:11
  241.1 0.1 reshape.10
  241.2 0.1 reduce_sum.36
  241.4 26.2 %convolution_reduce_fusion.2 = f32[384]{0:T(512)S(1)} fusion(f32[16384,1]{0,1:T(1,128)S(1)} %bitcast.20, f32[384,16384]{1,0:T(8,128)} %get-tuple-element.5, f32[384]{0:T(512)S(1)} %pmax.7), kind=kOutput, calls=%fused_computation.11 | convolution fusion | flops 81788928 | bytes 25234432 | tf_op jit(solution)/shard_map/dot_general | solution.py:28
  267.6 5.8 psum.29
  273.4 18.0 %fusion.9 = f32[1,16384]{1,0:T(1,128)S(1)} fusion(f32[384,1]{0,1:T(1,128)S(1)} %reshape.19, f32[384,16384]{1,0:T(8,128)} %get-tuple-element.5, f32[384]{0:T(512)S(1)} %pmax.7), kind=kOutput, calls=%fused_computation.20 | convolution fusion | flops 81788928 | bytes 25234432 | tf_op jit(solution)/shard_map/dot_general | solution.py:33
  291.4 31.3 %all-gather.1 = f32[131072]{0:T(1024)S(1)} all-gather(f32[16384]{0:T(1024)S(1)} %bitcast.18), channel_id=3, replica_groups=mesh['rows'=8,'code'=4] {'rows'}, dimensions={0}, use_global_device_ids=true | all-gather | bytes 589824 | tf_op jit(solution)/shard_map/all_gather | solution.py:11
  322.7 0.1 reshape.11
  322.8 0.1 reduce_sum.37
  323.0 26.2 %convolution_reduce_fusion.1 = f32[384]{0:T(512)S(1)} fusion(f32[16384,1]{0,1:T(1,128)S(1)} %bitcast.21, f32[384,16384]{1,0:T(8,128)} %get-tuple-element.5, f32[384]{0:T(512)S(1)} %pmax.7), kind=kOutput, calls=%fused_computation.10 | convolution fusion | flops 81788928 | bytes 25234432 | tf_op jit(solution)/shard_map/dot_general | solution.py:28
  349.2 5.9 psum.30
  355.1 18.0 %fusion.8 = f32[1,16384]{1,0:T(1,128)S(1)} fusion(f32[384,1]{0,1:T(1,128)S(1)} %reshape.23, f32[384,16384]{1,0:T(8,128)} %get-tuple-element.5, f32[384]{0:T(512)S(1)} %pmax.7), kind=kOutput, calls=%fused_computation.19 | convolution fusion | flops 81788928 | bytes 25234432 | tf_op jit(solution)/shard_map/dot_general | solution.py:33
  373.1 31.4 %all-gather.2 = f32[131072]{0:T(1024)S(1)} all-gather(f32[16384]{0:T(1024)S(1)} %bitcast.19), channel_id=4, replica_groups=mesh['rows'=8,'code'=4] {'rows'}, dimensions={0}, use_global_device_ids=true | all-gather | bytes 589824 | tf_op jit(solution)/shard_map/all_gather | solution.py:11
  404.5 0.1 reshape.12
  404.6 0.1 reduce_sum.38
  404.8 26.2 %convolution_reduce_fusion = f32[384]{0:T(512)S(1)} fusion(f32[16384,1]{0,1:T(1,128)S(1)} %bitcast.16, f32[384,16384]{1,0:T(8,128)} %get-tuple-element.5, f32[384]{0:T(512)S(1)} %pmax.7), kind=kOutput, calls=%fused_computation.9 | convolution fusion | flops 81788928 | bytes 25234432 | tf_op jit(solution)/shard_map/dot_general | solution.py:28
  431.0 5.7 psum.31
  436.6 11.9 %fusion.1 = f32[16384]{0:T(1024)} fusion(f32[16384]{0:T(1024)S(1)} %broadcast_divide_fusion, f32[384]{0:T(512)S(1)} %div.43, f32[384,16384]{1,0:T(8,128)} %get-tuple-element.5, f32[384]{0:T(512)S(1)} %pmax.7), kind=kLoop, calls=%fused_computation.4 | loop fusion | flops 25149440 | bytes 25299968 | tf_op jit(solution)/shard_map/reduce_sum | solution.py:37
  448.6 0.3 reduce-scatter.2.cloned.1.call-start
  448.9 14.9 %fusion.2 = f32[16384,256]{1,0:T(8,128)} fusion(bf16[384,256]{1,0:T(8,128)(2,1)S(1)} %copy-done, f32[16384]{0:T(1024)S(1)} %broadcast_divide_fusion, f32[384]{0:T(512)S(1)} %div.43, f32[384,16384]{1,0:T(8,128)} %get-tuple-element.5, f32[384]{0:T(512)S(1)} %pmax.7), kind=kOutput, calls=%fused_computation.5 | convolution fusion | flops 3246391296 | bytes 42208256 | tf_op jit(solution)/shard_map/nk,nd->kd/dot_general | solution.py:38
  463.9 0.6 dynamic-slice
  465.1 50.3 %all-reduce.3.cloned.1.call-done = f32[16384]{0:T(1024)} async-done(((f32[16384]{0:T(1024)}), f32[16384]{0:T(1024)}) %all-reduce.3.cloned.1.call-update) | async-done | bytes 65552
  515.4 1.3 broadcast_multiply_fusion
  516.7 285.0 %reduce-scatter.2.cloned.1.call-done = f32[2048,256]{1,0:T(8,128)} async-done(((f32[16384,256]{1,0:T(8,128)}), f32[2048,256]{1,0:T(8,128)}) %reduce-scatter.2.cloned.1.call-update) | async-done | bytes 2097168 | tf_op jit(solution)/shard_map/reduce_scatter | solution.py:45
  801.7 3.3 subtract_multiply_fusion
  (22 shorter events, 0.2 us)
Async XLA Ops:
  7.2 130.6 %copy-start = (bf16[384,256]{1,0:T(8,128)(2,1)S(1)}, bf16[384,256]{1,0:T(8,128)(2,1)}, u32[]{:S(2)}) copy-start(bf16[384,256]{1,0:T(8,128)(2,1)} %param.3) | copy-start | bytes 589828
  7.2 130.6 %all-gather.5.cloned.1.call-start = ((), (), s32[]{:S(2)}) async-start(), calls=%async_computation.1 | async-start | bytes 9437184 | tf_op jit(solution)/shard_map/all_gather | solution.py:21
  7.9 183.9 %copy-start.2 = (f32[384]{0:T(512)S(1)}, f32[384]{0:T(512)}, u32[]{:S(2)}) copy-start(f32[384]{0:T(512)} %param.5) | copy-start | bytes 4612
  7.9 507.5 %all-reduce.3.cloned.1.call-start = ((), (), s32[]{:S(2)}) async-start(), calls=%async_computation.3 | async-start | bytes 131072
  448.6 15.3 %copy-start.3 = (u32[32]{0:T(128)S(1)}, u32[32]{0:T(128)}, u32[]{:S(2)}) copy-start(u32[32]{0:T(128)} %constant.17) | copy-start | bytes 388
  448.6 353.1 %copy-start.1 = (bf16[2048,256]{1,0:T(8,128)(2,1)S(1)}, bf16[2048,256]{1,0:T(8,128)(2,1)}, u32[]{:S(2)}) copy-start(bf16[2048,256]{1,0:T(8,128)(2,1)} %param.4) | copy-start | bytes 3145732
  448.6 353.1 %reduce-scatter.2.cloned.1.call-start = ((), (), s32[]{:S(2)}) async-start(), calls=%async_computation.2 | async-start | bytes 18874368 | tf_op jit(solution)/shard_map/reduce_scatter | solution.py:45
Sparse Core Ops, SparseCore 0:
  10.1 127.6 all-gather.4
  448.7 66.6 all-reduce.2
  519.2 282.4 reduce-scatter.1
